TPU v7x, 256 devices: a whole 4x4x8 slice. The times are simulated.
256 devices in a mesh: rounds: 8 (over z), tiles: 32 (over y, x, core).
Axes of the slice: x: 4, y: 4, z: 8, core: 2. Of those that a mesh axis runs over, the one named last changes fastest.
Arguments:
- syndromes: int32 [8, 2, 8, 64, 64], P(None, None, 'rounds', 'tiles'), may hold values 0 or 1
- labels: int32 [2, 8], P(None, 'rounds'), may hold values from 0 to 1
- stab_gate: bfloat16 [64, 64, 512], P('tiles'), may hold values from -6 to 6
- bit_gate: float32 [512], replicated, may hold values from -6 to 6
- forget_bias: float32 [128], replicated, may hold values from -1 to 4
- conv_weight: bfloat16 [3, 3, 128, 512], replicated, may hold values from -0.375 to 0.375
- query: float32 [128], replicated, may hold values from -12 to 12
- readout_weight: float32 [128], replicated, may hold values from -6 to 6
Outputs:
- grad_conv: float32 [3, 3, 128, 512], replicated
- grad_stab: float32 [64, 64, 512], P('tiles')
- grad_bit: float32 [512], replicated
- grad_forget: float32 [128], replicated
- grad_query: float32 [128], replicated
- grad_readout: float32 [128], replicated
- loss: float32 [], replicated
All inputs are finite; a program needn't handle non-finite values. No bound on the sum of `syndromes` on one device may be relied on, other than what follows from the above.
Results may differ from a plain program's by a relative error of at most 0.014.
Values may be sent and summed in bfloat16 or wider, within the bound.
No kernel may reach another device: no remote copies, remote signals or barrier semaphores. Data moves between devices by JAX's collectives and lax.ppermute only.
A program may use at most 64 MiB of HBM per device.

v0:
```python
import math
import jax
import jax.numpy as jnp
from jax import lax
from jax.sharding import PartitionSpec as P


def with_halo(cells, sides, width):
    for axis, dim in sides:
        count = lax.axis_size(axis)
        ends = count - 1
        head = lax.slice_in_dim(cells, 0, width, axis=dim)
        tail = lax.slice_in_dim(cells, cells.shape[dim] - width, cells.shape[dim], axis=dim)
        cells = jnp.concatenate(
            [
                lax.ppermute(tail, axis, [(i, (i + 1) % count) for i in range(ends)]),
                cells,
                lax.ppermute(head, axis, [((i + 1) % count, i) for i in range(ends)]),
            ],
            axis=dim,
        )
    return cells


def make_patches(padded):
    row_count = padded.shape[1] - 2
    col_count = padded.shape[2] - 2
    pieces = [
        padded[:, a : a + row_count, b : b + col_count, :] for a in range(3) for b in range(3)
    ]
    return jnp.concatenate(pieces, axis=-1).reshape(-1, 9 * padded.shape[3])


def pad_columns(d_field):
    return jnp.pad(d_field, ((0, 0), (0, 0), (1, 1), (0, 0)))


def cell_forward(gate_input, cell_prev, channels):
    input_gate = jax.nn.sigmoid(gate_input[:, :channels])
    forget = jax.nn.sigmoid(gate_input[:, channels : 2 * channels])
    candidate = jnp.tanh(gate_input[:, 2 * channels : 3 * channels])
    output_gate = jax.nn.sigmoid(gate_input[:, 3 * channels :])
    cell_new = forget * cell_prev + input_gate * candidate
    hidden_new = (output_gate * jnp.tanh(cell_new)).astype(jnp.bfloat16)
    gate_values = jnp.concatenate([input_gate, forget, candidate, output_gate], axis=1)
    return (gate_values, cell_new, hidden_new)


def cell_backward(gate_values, cell_prev, cell_new, d_hidden, d_cell, channels):
    input_gate = gate_values[:, :channels]
    forget = gate_values[:, channels : 2 * channels]
    candidate = gate_values[:, 2 * channels : 3 * channels]
    output_gate = gate_values[:, 3 * channels :]
    squash = jnp.tanh(cell_new)
    d_total = d_cell + d_hidden * output_gate * (1.0 - squash * squash)
    d_gates = jnp.concatenate(
        [
            d_total * candidate * input_gate * (1.0 - input_gate),
            d_total * cell_prev * forget * (1.0 - forget),
            d_total * input_gate * (1.0 - candidate * candidate),
            d_hidden * squash * output_gate * (1.0 - output_gate),
        ],
        axis=1,
    ).astype(jnp.bfloat16)
    return (d_gates, d_total * forget)


def column_total(products, col_count, row_shift):
    result = products[:, :, 2 : 2 + col_count, row_shift, 0]
    for col_shift in range(1, 3):
        result = (
            result + products[:, :, 2 - col_shift : 2 - col_shift + col_count, row_shift, col_shift]
        )
    return result


def transpose_products(d_field, weight_matrix, channels):
    products = lax.dot_general(
        d_field, weight_matrix, (((3,), (1,)), ((), ())), preferred_element_type=jnp.float32
    )
    return products.reshape(d_field.shape[:3] + (3, 3, channels))


def per_device(
    syndromes, labels, stab_gate, bit_gate, forget_bias, conv_weight, query, readout_weight
):
    round_count, micro_count, shot_count, tile_rows, columns = syndromes.shape
    channels = conv_weight.shape[2]
    gate_units = conv_weight.shape[3]
    tile_sites = tile_rows * columns
    flat_rows = shot_count * tile_sites
    weight_matrix = conv_weight.reshape(9 * channels, gate_units)
    stab_rows = stab_gate.reshape(1, tile_sites, gate_units).astype(jnp.float32)
    forget_shift = jnp.concatenate(
        [jnp.zeros((channels,), jnp.float32), forget_bias, jnp.zeros((2 * channels,), jnp.float32)]
    )
    score_scale = 1.0 / math.sqrt(channels)
    field_shape = (shot_count, tile_rows, columns, channels)
    gate_shape = (shot_count, tile_rows, columns, gate_units)
    lead_tile = (lax.axis_index("tiles") == 0).astype(jnp.float32)

    def forward_round(recurrent, fired_bits):
        hidden_prev, cell_prev = recurrent
        hidden_rows = with_halo(hidden_prev, (("tiles", 1),), 1)
        hidden_pad = pad_columns(hidden_rows)
        gate_input = jnp.dot(
            make_patches(hidden_pad), weight_matrix, preferred_element_type=jnp.float32
        )
        gate_input = (
            gate_input.reshape(shot_count, tile_sites, gate_units)
            + stab_rows
            + fired_bits.astype(jnp.float32).reshape(shot_count, tile_sites, 1) * bit_gate
            + forget_shift
        )
        gate_values, cell_new, hidden_new = cell_forward(
            gate_input.reshape(flat_rows, gate_units), cell_prev, channels
        )
        return (
            (hidden_new.reshape(field_shape), cell_new),
            (hidden_pad, gate_values, cell_prev, cell_new, fired_bits),
        )

    def backward_round(state_carry, saved_items):
        d_hidden, d_cell, grad_weight, grad_stab_part, grad_fired, grad_keep = state_carry
        hidden_pad, gate_values, cell_prev, cell_new, fired_bits = saved_items
        d_gates, d_cell_prev = cell_backward(
            gate_values, cell_prev, cell_new, d_hidden, d_cell, channels
        )
        grad_weight = grad_weight + lax.dot_general(
            make_patches(hidden_pad),
            d_gates,
            (((0,), (0,)), ((), ())),
            preferred_element_type=jnp.float32,
        )
        grad_stab_part = grad_stab_part + jnp.sum(
            d_gates.reshape(shot_count, tile_sites, gate_units).astype(jnp.float32), axis=0
        )
        fired_row = fired_bits.astype(jnp.bfloat16).reshape(1, flat_rows)
        grad_fired = grad_fired + jnp.dot(fired_row, d_gates, preferred_element_type=jnp.float32)[0]
        grad_keep = grad_keep + jnp.sum(
            d_gates[:, channels : 2 * channels].astype(jnp.float32), axis=0
        )
        d_field = d_gates.reshape(gate_shape)
        d_rows = with_halo(d_field, (("tiles", 1),), 1)
        products = transpose_products(pad_columns(d_rows), weight_matrix, channels)
        d_hidden_prev = column_total(products[:, 2 : 2 + tile_rows], columns, 0)
        for row_shift in range(1, 3):
            d_hidden_prev = d_hidden_prev + column_total(
                products[:, 2 - row_shift : 2 - row_shift + tile_rows], columns, row_shift
            )
        return (
            (
                d_hidden_prev.reshape(flat_rows, channels),
                d_cell_prev,
                grad_weight,
                grad_stab_part,
                grad_fired,
                grad_keep,
            ),
            None,
        )

    def one_batch(totals, inputs):
        fired_rounds, batch_labels = inputs
        initial = (
            jnp.zeros(field_shape, jnp.bfloat16),
            jnp.zeros((flat_rows, channels), jnp.float32),
        )
        (hidden_last, unused_cell), saved = lax.scan(forward_round, initial, fired_rounds)
        hidden_full = hidden_last.astype(jnp.float32).reshape(shot_count, tile_sites, channels)
        scores = jnp.sum(hidden_full * query, axis=2) * score_scale
        exp_score = jnp.exp(scores)
        part_total = jnp.sum(exp_score, axis=1)
        part_numer = jnp.sum(exp_score[..., None] * hidden_full, axis=1)
        total_exp, numer = lax.psum((part_total, part_numer), "tiles")
        pooled = numer / total_exp[:, None]
        logit_value = jnp.sum(pooled * readout_weight, axis=1)
        targets = batch_labels.astype(jnp.float32)
        loss_part = jnp.sum(jax.nn.softplus(logit_value) - targets * logit_value)
        d_logit = jax.nn.sigmoid(logit_value) - targets
        d_pooled = d_logit[:, None] * readout_weight
        weight = exp_score / total_exp[:, None]
        d_score = weight * (
            jnp.sum(hidden_full * d_pooled[:, None, :], axis=2)
            - jnp.sum(pooled * d_pooled, axis=1)[:, None]
        )
        final_grad = (
            weight[..., None] * d_pooled[:, None, :] + d_score[..., None] * query * score_scale
        )
        query_part = score_scale * jnp.sum(d_score[..., None] * hidden_full, axis=(0, 1))
        readout_part = jnp.sum(d_logit[:, None] * pooled, axis=0)
        grad_weight, grad_stab_part, grad_fired, grad_keep, grad_query, grad_readout, loss_total = (
            totals
        )
        start_back = (
            final_grad.reshape(flat_rows, channels),
            jnp.zeros((flat_rows, channels), jnp.float32),
            grad_weight,
            grad_stab_part,
            grad_fired,
            grad_keep,
        )
        back_state, unused_out = lax.scan(backward_round, start_back, saved, reverse=True)
        return (
            (
                back_state[2],
                back_state[3],
                back_state[4],
                back_state[5],
                grad_query + query_part,
                grad_readout + readout_part,
                loss_total + loss_part,
            ),
            None,
        )

    zero_totals = (
        jnp.zeros((9 * channels, gate_units), jnp.float32),
        jnp.zeros((tile_sites, gate_units), jnp.float32),
        jnp.zeros((gate_units,), jnp.float32),
        jnp.zeros((channels,), jnp.float32),
        jnp.zeros((channels,), jnp.float32),
        jnp.zeros((channels,), jnp.float32),
        jnp.zeros((), jnp.float32),
    )
    batch_inputs = (jnp.swapaxes(syndromes, 0, 1), labels)
    sums, unused_out = lax.scan(one_batch, zero_totals, batch_inputs)
    grad_weight, grad_stab_part, grad_fired, grad_keep, grad_query, grad_readout, loss_total = sums
    stab_total = lax.psum(grad_stab_part.astype(jnp.bfloat16), "rounds").astype(jnp.float32)
    totals = lax.psum(
        (
            grad_weight,
            grad_fired,
            grad_keep,
            grad_query,
            grad_readout * lead_tile,
            loss_total * lead_tile,
        ),
        ("rounds", "tiles"),
    )
    return (
        totals[0].reshape(3, 3, channels, gate_units),
        stab_total.reshape(tile_rows, columns, gate_units),
        totals[1],
        totals[2],
        totals[3],
        totals[4],
        totals[5],
    )


def solution(mesh):
    in_specs = (
        P(None, None, "rounds", "tiles", None),
        P(None, "rounds"),
        P("tiles", None, None),
        P(),
        P(),
        P(),
        P(),
        P(),
    )
    out_specs = (P(), P("tiles", None, None), P(), P(), P(), P(), P())
    return jax.shard_map(
        per_device, mesh=mesh, in_specs=in_specs, out_specs=out_specs, check_vma=False
    )
```

profile of v0, /device:TPU:2, one launch (start us, length us, event | category | flops | bytes accessed | tf_op | source)
XLA Modules:
  0.0 1043.6 jit_solution(17618227137616668080)
XLA Ops:
  11.9 661.5 %while.108 = (s32[]{:T(128)}, f32[1152,512]{1,0:T(8,128)S(1)}, f32[128,512]{1,0:T(8,128)}, f32[512]{0:T(512)S(1)}, f32[128]{0:T(128)}, /*index=5*/f32[128]{0:T(1...) while((s32[]{:T(128)}, f32[1152,512]{1,0:T(8,128)S(1)}, ...), condition=%wide.region_15.16_spmd.clone, body=%wide.region_0.15_spmd.clone.sunk | while | flops 621755008 | bytes 24381452 | solution.py:227
  13.2 88.8 %while.109 = (s32[]{:T(128)}, bf16[1,2,64,128]{3,2,1,0:T(8,128)(2,1)S(1)}, f32[128,128]{1,0:T(8,128)S(1)}, bf16[8,1,4,66,128]{4,3,2,1,0:T(8,128)(2,1)}, f32[8,12...) while((s32[]{:T(128)}, ...), condition=%wide.region_2.2_spmd.clone, body=%wide.region_1.1_spmd.clone.sunk | while | flops 152739968 | bytes 4702967 | solution.py:169
  103.6 68.7 %all-reduce.5 = (f32[]{:T(128)}, f32[1,128]{1,0:T(1,128)S(1)}) all-reduce(f32[]{:T(128)} %get-tuple-element.1439, f32[1,128]{1,0:T(1,128)S(1)} %bitcast.186), channel_id=1, replica_groups=mesh['rounds'=8,'tiles'=32] {'tiles'}, use_global_device_ids=true, to_apply=%region_5.5 | all-reduce | flops 129 | bytes 1032 | tf_op jit(solution)/shard_map/while/body/eval_jaxpr/psum | solution.py:175
  185.9 148.6 %while.110 = (s32[]{:T(128)}, f32[128,128]{1,0:T(8,128)S(1)}, f32[128,128]{1,0:T(8,128)}, f32[1152,512]{1,0:T(8,128)S(1)}, f32[128,512]{1,0:T(8,128)}, /*index=5...) while((s32[]{:T(128)}, f32[128,128]{1,0:T(8,128)S(1)}, ...), condition=%wide.region_13.13_spmd.clone, body=%wide.region_11.12_spmd.clone.sunk | while | flops 468750976 | bytes 19420224 | solution.py:203
  189.8 6.0 collective-permute-start.2
  210.5 3.6 collective-permute-start.2
  228.7 3.6 collective-permute-start.2
  247.1 3.6 collective-permute-start.2
  265.3 3.6 collective-permute-start.2
  283.6 3.6 collective-permute-start.2
  301.9 3.6 collective-permute-start.2
  320.1 3.6 collective-permute-start.2
  335.8 100.8 %while.109 = (s32[]{:T(128)}, bf16[1,2,64,128]{3,2,1,0:T(8,128)(2,1)S(1)}, f32[128,128]{1,0:T(8,128)S(1)}, bf16[8,1,4,66,128]{4,3,2,1,0:T(8,128)(2,1)}, f32[8,12...) while((s32[]{:T(128)}, ...), condition=%wide.region_2.2_spmd.clone, body=%wide.region_1.1_spmd.clone.sunk | while | flops 152739968 | bytes 4702967 | solution.py:169
  335.9 3.6 collective-permute-start
  350.5 4.8 collective-permute-start.1
  362.1 5.8 collective-permute-start.1
  374.6 5.8 collective-permute-start.1
  387.2 5.8 collective-permute-start.1
  399.7 5.8 collective-permute-start.1
  412.3 6.3 collective-permute-start.1
  425.4 6.3 collective-permute-start.1
  438.3 72.4 %all-reduce.5 = (f32[]{:T(128)}, f32[1,128]{1,0:T(1,128)S(1)}) all-reduce(f32[]{:T(128)} %get-tuple-element.1439, f32[1,128]{1,0:T(1,128)S(1)} %bitcast.186), channel_id=1, replica_groups=mesh['rounds'=8,'tiles'=32] {'tiles'}, use_global_device_ids=true, to_apply=%region_5.5 | all-reduce | flops 129 | bytes 1032 | tf_op jit(solution)/shard_map/while/body/eval_jaxpr/psum | solution.py:175
  524.8 148.6 %while.110 = (s32[]{:T(128)}, f32[128,128]{1,0:T(8,128)S(1)}, f32[128,128]{1,0:T(8,128)}, f32[1152,512]{1,0:T(8,128)S(1)}, f32[128,512]{1,0:T(8,128)}, /*index=5...) while((s32[]{:T(128)}, f32[128,128]{1,0:T(8,128)S(1)}, ...), condition=%wide.region_13.13_spmd.clone, body=%wide.region_11.12_spmd.clone.sunk | while | flops 468750976 | bytes 19420224 | solution.py:203
  528.7 6.0 collective-permute-start.2
  549.4 3.6 collective-permute-start.2
  567.6 3.6 collective-permute-start.2
  585.9 3.6 collective-permute-start.2
  604.2 3.6 collective-permute-start.2
  622.5 3.6 collective-permute-start.2
  640.8 3.6 collective-permute-start.2
  676.7 94.3 %all-reduce.3 = (f32[512]{0:T(512)}, f32[128]{0:T(128)}, f32[128]{0:T(128)}, f32[128]{0:T(128)}, f32[]{:T(128)}) all-reduce(f32[512]{0:T(512)S(1)} %get-tuple-element.1688, f32[128]{0:T(128)S(1)} %copy-done.13, f32[128]{0:T(128)} %get-tuple-element.1690, ...), channel_id=1, replica_groups=mesh['rounds'=8,'tiles'=32] {'rounds','tiles'}, use_global_device_ids=true, to_apply=%region_18.19 | all-reduce | flops 897 | bytes 7176 | tf_op jit(solution)/shard_map/psum | solution.py:230
  772.7 260.7 %all-reduce.9.cloned.1.call-done = f32[3,3,128,512]{3,2,1,0:T(8,128)} async-done(((f32[3,3,128,512]{3,2,1,0:T(8,128)}), f32[3,3,128,512]{3,2,1,0:T(8,128)}) %all-reduce.9.cloned.1.call-update) | async-done | bytes 2359312 | tf_op jit(solution)/shard_map/psum | solution.py:230
  (1202 shorter events, 414.5 us)
Async XLA Ops:
  7.2 763.9 %all-reduce.11.cloned.1.call-start = ((), (), s32[]{:S(2)}) async-start(), calls=%async_computation.1 | async-start | bytes 262144 | tf_op jit(solution)/shard_map/psum | solution.py:229
  189.8 15.2 %collective-permute-start.2 = (bf16[1,1,64,512]{3,2,1,0:T(8,128)(2,1)}, bf16[1,1,64,512]{3,2,1,0:T(8,128)(2,1)}, u32[]{:S(2)}, u32[]{:S(2)}) collective-permute-start(bf16[1,1,64,512]{3,2,1,0:T(8,128)(2,1)} %get-tuple-element.1494), channel_id=1, source_target_pairs={{1,0},{2,1},{3,2},{4,3},{5,4},{6,5},{7,6},{8,7},{9,8},{10,9},{11,1... | collective-permute-start | bytes 196616 | tf_op jit(solution)/shard_map/while/body/eval_jaxpr/while/body/eval_jaxpr/ppermute | solution.py:18
  195.8 9.2 collective-permute-start.3
  210.5 12.8 %collective-permute-start.2 = (bf16[1,1,64,512]{3,2,1,0:T(8,128)(2,1)}, bf16[1,1,64,512]{3,2,1,0:T(8,128)(2,1)}, u32[]{:S(2)}, u32[]{:S(2)}) collective-permute-start(bf16[1,1,64,512]{3,2,1,0:T(8,128)(2,1)} %get-tuple-element.1494), channel_id=1, source_target_pairs={{1,0},{2,1},{3,2},{4,3},{5,4},{6,5},{7,6},{8,7},{9,8},{10,9},{11,1... | collective-permute-start | bytes 196616 | tf_op jit(solution)/shard_map/while/body/eval_jaxpr/while/body/eval_jaxpr/ppermute | solution.py:18
  214.1 9.2 collective-permute-start.3
  228.7 12.9 %collective-permute-start.2 = (bf16[1,1,64,512]{3,2,1,0:T(8,128)(2,1)}, bf16[1,1,64,512]{3,2,1,0:T(8,128)(2,1)}, u32[]{:S(2)}, u32[]{:S(2)}) collective-permute-start(bf16[1,1,64,512]{3,2,1,0:T(8,128)(2,1)} %get-tuple-element.1494), channel_id=1, source_target_pairs={{1,0},{2,1},{3,2},{4,3},{5,4},{6,5},{7,6},{8,7},{9,8},{10,9},{11,1... | collective-permute-start | bytes 196616 | tf_op jit(solution)/shard_map/while/body/eval_jaxpr/while/body/eval_jaxpr/ppermute | solution.py:18
  232.4 9.2 collective-permute-start.3
  247.1 12.8 %collective-permute-start.2 = (bf16[1,1,64,512]{3,2,1,0:T(8,128)(2,1)}, bf16[1,1,64,512]{3,2,1,0:T(8,128)(2,1)}, u32[]{:S(2)}, u32[]{:S(2)}) collective-permute-start(bf16[1,1,64,512]{3,2,1,0:T(8,128)(2,1)} %get-tuple-element.1494), channel_id=1, source_target_pairs={{1,0},{2,1},{3,2},{4,3},{5,4},{6,5},{7,6},{8,7},{9,8},{10,9},{11,1... | collective-permute-start | bytes 196616 | tf_op jit(solution)/shard_map/while/body/eval_jaxpr/while/body/eval_jaxpr/ppermute | solution.py:18
  250.7 9.2 collective-permute-start.3
  265.3 12.8 %collective-permute-start.2 = (bf16[1,1,64,512]{3,2,1,0:T(8,128)(2,1)}, bf16[1,1,64,512]{3,2,1,0:T(8,128)(2,1)}, u32[]{:S(2)}, u32[]{:S(2)}) collective-permute-start(bf16[1,1,64,512]{3,2,1,0:T(8,128)(2,1)} %get-tuple-element.1494), channel_id=1, source_target_pairs={{1,0},{2,1},{3,2},{4,3},{5,4},{6,5},{7,6},{8,7},{9,8},{10,9},{11,1... | collective-permute-start | bytes 196616 | tf_op jit(solution)/shard_map/while/body/eval_jaxpr/while/body/eval_jaxpr/ppermute | solution.py:18
  269.0 9.2 collective-permute-start.3
  283.6 12.8 %collective-permute-start.2 = (bf16[1,1,64,512]{3,2,1,0:T(8,128)(2,1)}, bf16[1,1,64,512]{3,2,1,0:T(8,128)(2,1)}, u32[]{:S(2)}, u32[]{:S(2)}) collective-permute-start(bf16[1,1,64,512]{3,2,1,0:T(8,128)(2,1)} %get-tuple-element.1494), channel_id=1, source_target_pairs={{1,0},{2,1},{3,2},{4,3},{5,4},{6,5},{7,6},{8,7},{9,8},{10,9},{11,1... | collective-permute-start | bytes 196616 | tf_op jit(solution)/shard_map/while/body/eval_jaxpr/while/body/eval_jaxpr/ppermute | solution.py:18
  287.2 9.2 collective-permute-start.3
  301.9 12.8 %collective-permute-start.2 = (bf16[1,1,64,512]{3,2,1,0:T(8,128)(2,1)}, bf16[1,1,64,512]{3,2,1,0:T(8,128)(2,1)}, u32[]{:S(2)}, u32[]{:S(2)}) collective-permute-start(bf16[1,1,64,512]{3,2,1,0:T(8,128)(2,1)} %get-tuple-element.1494), channel_id=1, source_target_pairs={{1,0},{2,1},{3,2},{4,3},{5,4},{6,5},{7,6},{8,7},{9,8},{10,9},{11,1... | collective-permute-start | bytes 196616 | tf_op jit(solution)/shard_map/while/body/eval_jaxpr/while/body/eval_jaxpr/ppermute | solution.py:18
  320.1 12.8 %collective-permute-start.2 = (bf16[1,1,64,512]{3,2,1,0:T(8,128)(2,1)}, bf16[1,1,64,512]{3,2,1,0:T(8,128)(2,1)}, u32[]{:S(2)}, u32[]{:S(2)}) collective-permute-start(bf16[1,1,64,512]{3,2,1,0:T(8,128)(2,1)} %get-tuple-element.1494), channel_id=1, source_target_pairs={{1,0},{2,1},{3,2},{4,3},{5,4},{6,5},{7,6},{8,7},{9,8},{10,9},{11,1... | collective-permute-start | bytes 196616 | tf_op jit(solution)/shard_map/while/body/eval_jaxpr/while/body/eval_jaxpr/ppermute | solution.py:18
  323.8 9.2 collective-permute-start.3
  528.7 15.2 %collective-permute-start.2 = (bf16[1,1,64,512]{3,2,1,0:T(8,128)(2,1)}, bf16[1,1,64,512]{3,2,1,0:T(8,128)(2,1)}, u32[]{:S(2)}, u32[]{:S(2)}) collective-permute-start(bf16[1,1,64,512]{3,2,1,0:T(8,128)(2,1)} %get-tuple-element.1494), channel_id=1, source_target_pairs={{1,0},{2,1},{3,2},{4,3},{5,4},{6,5},{7,6},{8,7},{9,8},{10,9},{11,1... | collective-permute-start | bytes 196616 | tf_op jit(solution)/shard_map/while/body/eval_jaxpr/while/body/eval_jaxpr/ppermute | solution.py:18
  534.7 9.2 collective-permute-start.3
  549.4 12.8 %collective-permute-start.2 = (bf16[1,1,64,512]{3,2,1,0:T(8,128)(2,1)}, bf16[1,1,64,512]{3,2,1,0:T(8,128)(2,1)}, u32[]{:S(2)}, u32[]{:S(2)}) collective-permute-start(bf16[1,1,64,512]{3,2,1,0:T(8,128)(2,1)} %get-tuple-element.1494), channel_id=1, source_target_pairs={{1,0},{2,1},{3,2},{4,3},{5,4},{6,5},{7,6},{8,7},{9,8},{10,9},{11,1... | collective-permute-start | bytes 196616 | tf_op jit(solution)/shard_map/while/body/eval_jaxpr/while/body/eval_jaxpr/ppermute | solution.py:18
  553.0 9.2 collective-permute-start.3
  567.6 12.8 %collective-permute-start.2 = (bf16[1,1,64,512]{3,2,1,0:T(8,128)(2,1)}, bf16[1,1,64,512]{3,2,1,0:T(8,128)(2,1)}, u32[]{:S(2)}, u32[]{:S(2)}) collective-permute-start(bf16[1,1,64,512]{3,2,1,0:T(8,128)(2,1)} %get-tuple-element.1494), channel_id=1, source_target_pairs={{1,0},{2,1},{3,2},{4,3},{5,4},{6,5},{7,6},{8,7},{9,8},{10,9},{11,1... | collective-permute-start | bytes 196616 | tf_op jit(solution)/shard_map/while/body/eval_jaxpr/while/body/eval_jaxpr/ppermute | solution.py:18
  571.3 9.2 collective-permute-start.3
  585.9 12.8 %collective-permute-start.2 = (bf16[1,1,64,512]{3,2,1,0:T(8,128)(2,1)}, bf16[1,1,64,512]{3,2,1,0:T(8,128)(2,1)}, u32[]{:S(2)}, u32[]{:S(2)}) collective-permute-start(bf16[1,1,64,512]{3,2,1,0:T(8,128)(2,1)} %get-tuple-element.1494), channel_id=1, source_target_pairs={{1,0},{2,1},{3,2},{4,3},{5,4},{6,5},{7,6},{8,7},{9,8},{10,9},{11,1... | collective-permute-start | bytes 196616 | tf_op jit(solution)/shard_map/while/body/eval_jaxpr/while/body/eval_jaxpr/ppermute | solution.py:18
  589.6 9.2 collective-permute-start.3
  604.2 12.8 %collective-permute-start.2 = (bf16[1,1,64,512]{3,2,1,0:T(8,128)(2,1)}, bf16[1,1,64,512]{3,2,1,0:T(8,128)(2,1)}, u32[]{:S(2)}, u32[]{:S(2)}) collective-permute-start(bf16[1,1,64,512]{3,2,1,0:T(8,128)(2,1)} %get-tuple-element.1494), channel_id=1, source_target_pairs={{1,0},{2,1},{3,2},{4,3},{5,4},{6,5},{7,6},{8,7},{9,8},{10,9},{11,1... | collective-permute-start | bytes 196616 | tf_op jit(solution)/shard_map/while/body/eval_jaxpr/while/body/eval_jaxpr/ppermute | solution.py:18
  607.9 9.2 collective-permute-start.3
  622.5 12.8 %collective-permute-start.2 = (bf16[1,1,64,512]{3,2,1,0:T(8,128)(2,1)}, bf16[1,1,64,512]{3,2,1,0:T(8,128)(2,1)}, u32[]{:S(2)}, u32[]{:S(2)}) collective-permute-start(bf16[1,1,64,512]{3,2,1,0:T(8,128)(2,1)} %get-tuple-element.1494), channel_id=1, source_target_pairs={{1,0},{2,1},{3,2},{4,3},{5,4},{6,5},{7,6},{8,7},{9,8},{10,9},{11,1... | collective-permute-start | bytes 196616 | tf_op jit(solution)/shard_map/while/body/eval_jaxpr/while/body/eval_jaxpr/ppermute | solution.py:18
  626.1 9.2 collective-permute-start.3
  640.8 12.8 %collective-permute-start.2 = (bf16[1,1,64,512]{3,2,1,0:T(8,128)(2,1)}, bf16[1,1,64,512]{3,2,1,0:T(8,128)(2,1)}, u32[]{:S(2)}, u32[]{:S(2)}) collective-permute-start(bf16[1,1,64,512]{3,2,1,0:T(8,128)(2,1)} %get-tuple-element.1494), channel_id=1, source_target_pairs={{1,0},{2,1},{3,2},{4,3},{5,4},{6,5},{7,6},{8,7},{9,8},{10,9},{11,1... | collective-permute-start | bytes 196616 | tf_op jit(solution)/shard_map/while/body/eval_jaxpr/while/body/eval_jaxpr/ppermute | solution.py:18
  659.0 12.8 %collective-permute-start.2 = (bf16[1,1,64,512]{3,2,1,0:T(8,128)(2,1)}, bf16[1,1,64,512]{3,2,1,0:T(8,128)(2,1)}, u32[]{:S(2)}, u32[]{:S(2)}) collective-permute-start(bf16[1,1,64,512]{3,2,1,0:T(8,128)(2,1)} %get-tuple-element.1494), channel_id=1, source_target_pairs={{1,0},{2,1},{3,2},{4,3},{5,4},{6,5},{7,6},{8,7},{9,8},{10,9},{11,1... | collective-permute-start | bytes 196616 | tf_op jit(solution)/shard_map/while/body/eval_jaxpr/while/body/eval_jaxpr/ppermute | solution.py:18
  662.7 9.2 collective-permute-start.3
  675.3 358.1 %all-reduce.9.cloned.1.call-start = ((), (), s32[]{:S(2)}) async-start(), calls=%async_computation | async-start | bytes 4718592 | tf_op jit(solution)/shard_map/psum | solution.py:230
  (214 other events, 1059.1 us)
Sparse Core Ops, SparseCore 0:
  675.4 90.3 all-reduce.10
  771.8 261.6 all-reduce.8
where the time goes:
time: 1050 us; the launch traced here: 1040 us
  waiting for transfers between devices  279 us (27%)
  blocking collectives  235 us (22%)
  starting transfers between devices  189 us (18%)
  other arithmetic  168 us (16%)
  matrix products  77.6 us (7%)
  local copies, waits for them, and re-layouts  65.3 us (6%)
  loops' own time  15.4 us (1%)
  between operations  14.1 us (1%)
    psum x1, waiting for transfers between devices, per_device(): lax.psum((grad_weight, grad_fired, grad_keep, grad_query, grad_readout *...  261 us
    psum x2, blocking collectives, one_batch(): total_exp, numer = lax.psum((part_total, part_numer), 'tiles')  141 us
    ppermute x32, starting transfers between devices, with_halo(): lax.ppermute(head, axis, [((i + 1) % count, i) for i in range(ends)])  95.1 us
    psum x1, blocking collectives, per_device(): lax.psum((grad_weight, grad_fired, grad_keep, grad_query, grad_readout *...  94.3 us
    ppermute x32, starting transfers between devices, with_halo(): lax.ppermute(tail, axis, [(i, (i + 1) % count) for i in range(ends)])  93.7 us
    dynamic_update_slice x48, other arithmetic, one_batch(): lax.scan(forward_round, initial, fired_rounds)  33.1 us
    squeeze x32, local copies, waits for them, and re-layouts, one_batch(): lax.scan(backward_round, start_back, saved, reverse=True)  29.9 us
    add x16, other arithmetic, backward_round(): grad_stab_part + jnp.sum(d_gates.reshape(shot_count, tile_sites, gate_uni...  28.7 us
  transfers between devices with their start and end apart: 66, of which 15 were waited for; matrix products, arithmetic and copies ran while one was open for 12% of the time, Pallas kernels for 0%

commit v1 on v0

--- a/solution.py
+++ b/solution.py
@@ -227,7 +227,9 @@
     sums, unused_out = lax.scan(one_batch, zero_totals, batch_inputs)
     grad_weight, grad_stab_part, grad_fired, grad_keep, grad_query, grad_readout, loss_total = sums
     stab_total = lax.psum(grad_stab_part.astype(jnp.bfloat16), "rounds").astype(jnp.float32)
-    totals = lax.psum(
+    _arrange_face = lambda axis_name, m, net_axis: lax.psum(lax.psum(m, net_axis), axis_name)
+    totals = _arrange_face(
+        "rounds",
         (
             grad_weight,
             grad_fired,
@@ -236,7 +238,7 @@
             grad_readout * lead_tile,
             loss_total * lead_tile,
         ),
-        ("rounds", "tiles"),
+        "tiles",
     )
     return (
         totals[0].reshape(3, 3, channels, gate_units),

time: 1050 us -> 987 us (0.940)
  waiting for transfers between devices: 279 us -> 227 us
  blocking collectives: 235 us -> 222 us
    psum x1 -> x2, waiting for transfers between devices: 261 us -> 210 us  [the longest x1 133 us: per_device(): lax.psum(m, net_axis)]
    psum x1 -> x2, blocking collectives: 94.3 us -> 80.5 us  [the longest x1 62.4 us: per_device(): lax.psum(m, net_axis)]
  transfers between devices with their start and end apart: 66 -> 67, of which waited for: 15 -> 17; matrix products, arithmetic and copies ran while one was open for 12% -> 13% of each run, Pallas kernels for 0% -> 0%
where the time goes in v1:
time: 987 us; the launch traced here: 980 us
  waiting for transfers between devices  227 us (23%)
  blocking collectives  222 us (22%)
  starting transfers between devices  189 us (19%)
  other arithmetic  167 us (17%)
  matrix products  77.6 us (8%)
  local copies, waits for them, and re-layouts  66.7 us (7%)
  loops' own time  17.1 us (2%)
  between operations  13.8 us (1%)
    psum x2, blocking collectives, one_batch(): total_exp, numer = lax.psum((part_total, part_numer), 'tiles')  141 us
    psum x1, waiting for transfers between devices, per_device(): lax.psum(m, net_axis)  133 us
    ppermute x32, starting transfers between devices, with_halo(): lax.ppermute(head, axis, [((i + 1) % count, i) for i in range(ends)])  95.2 us
    ppermute x32, starting transfers between devices, with_halo(): lax.ppermute(tail, axis, [(i, (i + 1) % count) for i in range(ends)])  93.7 us
    psum x1, waiting for transfers between devices, per_device(): lax.psum(lax.psum(m, net_axis), axis_name)  76.9 us
    psum x1, blocking collectives, per_device(): lax.psum(m, net_axis)  62.4 us
    dynamic_update_slice x48, other arithmetic, one_batch(): lax.scan(forward_round, initial, fired_rounds)  33.1 us
    squeeze x32, local copies, waits for them, and re-layouts, one_batch(): lax.scan(backward_round, start_back, saved, reverse=True)  29.9 us
  transfers between devices with their start and end apart: 67, of which 17 were waited for; matrix products, arithmetic and copies ran while one was open for 13% of the time, Pallas kernels for 0%

profile of v1, /device:TPU:2, one launch (start us, length us, event | category | flops | bytes accessed | tf_op | source)
XLA Modules:
  0.0 980.3 jit_solution(2812449524779749377)
XLA Ops:
  11.9 662.5 %while.108 = (s32[]{:T(128)}, f32[1152,512]{1,0:T(8,128)S(1)}, f32[128,512]{1,0:T(8,128)}, f32[512]{0:T(512)S(1)}, f32[128]{0:T(128)}, /*index=5*/f32[128]{0:T(1...) while((s32[]{:T(128)}, f32[1152,512]{1,0:T(8,128)S(1)}, ...), condition=%wide.region_15.16_spmd.clone, body=%wide.region_0.15_spmd.clone.sunk | while | flops 621755008 | bytes 24381452 | solution.py:227
  13.2 88.8 %while.109 = (s32[]{:T(128)}, bf16[1,2,64,128]{3,2,1,0:T(8,128)(2,1)S(1)}, f32[128,128]{1,0:T(8,128)S(1)}, bf16[8,1,4,66,128]{4,3,2,1,0:T(8,128)(2,1)}, f32[8,12...) while((s32[]{:T(128)}, ...), condition=%wide.region_2.2_spmd.clone, body=%wide.region_1.1_spmd.clone.sunk | while | flops 152739968 | bytes 4702967 | solution.py:169
  103.6 68.7 %all-reduce.6 = (f32[]{:T(128)}, f32[1,128]{1,0:T(1,128)S(1)}) all-reduce(f32[]{:T(128)} %get-tuple-element.1444, f32[1,128]{1,0:T(1,128)S(1)} %bitcast.186), channel_id=1, replica_groups=mesh['rounds'=8,'tiles'=32] {'tiles'}, use_global_device_ids=true, to_apply=%region_5.5 | all-reduce | flops 129 | bytes 1032 | tf_op jit(solution)/shard_map/while/body/eval_jaxpr/psum | solution.py:175
  186.5 148.4 %while.110 = (s32[]{:T(128)}, f32[128,128]{1,0:T(8,128)S(1)}, f32[128,128]{1,0:T(8,128)}, f32[1152,512]{1,0:T(8,128)S(1)}, f32[128,512]{1,0:T(8,128)}, /*index=5...) while((s32[]{:T(128)}, f32[128,128]{1,0:T(8,128)S(1)}, ...), condition=%wide.region_13.13_spmd.clone, body=%wide.region_11.12_spmd.clone.sunk | while | flops 468750976 | bytes 19420224 | solution.py:203
  190.4 6.0 collective-permute-start.2
  229.3 3.6 collective-permute-start.2
  247.6 3.6 collective-permute-start.2
  265.8 3.6 collective-permute-start.2
  284.0 3.6 collective-permute-start.2
  320.6 3.6 collective-permute-start.2
  336.3 100.8 %while.109 = (s32[]{:T(128)}, bf16[1,2,64,128]{3,2,1,0:T(8,128)(2,1)S(1)}, f32[128,128]{1,0:T(8,128)S(1)}, bf16[8,1,4,66,128]{4,3,2,1,0:T(8,128)(2,1)}, f32[8,12...) while((s32[]{:T(128)}, ...), condition=%wide.region_2.2_spmd.clone, body=%wide.region_1.1_spmd.clone.sunk | while | flops 152739968 | bytes 4702967 | solution.py:169
  336.3 3.6 collective-permute-start
  351.0 4.8 collective-permute-start.1
  362.5 5.7 collective-permute-start.1
  375.1 5.8 collective-permute-start.1
  387.7 5.7 collective-permute-start.1
  400.2 5.8 collective-permute-start.1
  412.8 6.4 collective-permute-start.1
  425.9 6.3 collective-permute-start.1
  438.7 72.4 %all-reduce.6 = (f32[]{:T(128)}, f32[1,128]{1,0:T(1,128)S(1)}) all-reduce(f32[]{:T(128)} %get-tuple-element.1444, f32[1,128]{1,0:T(1,128)S(1)} %bitcast.186), channel_id=1, replica_groups=mesh['rounds'=8,'tiles'=32] {'tiles'}, use_global_device_ids=true, to_apply=%region_5.5 | all-reduce | flops 129 | bytes 1032 | tf_op jit(solution)/shard_map/while/body/eval_jaxpr/psum | solution.py:175
  525.9 148.4 %while.110 = (s32[]{:T(128)}, f32[128,128]{1,0:T(8,128)S(1)}, f32[128,128]{1,0:T(8,128)}, f32[1152,512]{1,0:T(8,128)S(1)}, f32[128,512]{1,0:T(8,128)}, /*index=5...) while((s32[]{:T(128)}, f32[128,128]{1,0:T(8,128)S(1)}, ...), condition=%wide.region_13.13_spmd.clone, body=%wide.region_11.12_spmd.clone.sunk | while | flops 468750976 | bytes 19420224 | solution.py:203
  529.8 6.0 collective-permute-start.2
  550.4 3.6 collective-permute-start.2
  568.6 3.6 collective-permute-start.2
  586.9 3.6 collective-permute-start.2
  605.2 3.6 collective-permute-start.2
  623.4 3.6 collective-permute-start.2
  660.0 3.6 collective-permute-start.2
  677.5 133.1 %all-reduce.11.cloned.1.call-done = f32[1152,512]{1,0:T(8,128)} async-done(((f32[1152,512]{1,0:T(8,128)}), f32[1152,512]{1,0:T(8,128)}) %all-reduce.11.cloned.1.call-update) | async-done | bytes 2359312 | tf_op jit(solution)/shard_map/psum | solution.py:230
  811.3 62.4 %all-reduce.3 = (f32[512]{0:T(512)S(1)}, f32[128]{0:T(128)S(1)}, f32[128]{0:T(128)S(1)}, f32[128]{0:T(128)S(1)}, f32[]{:T(128)}) all-reduce(f32[512]{0:T(512)S(1)} %get-tuple-element.1697, f32[128]{0:T(128)S(1)} %copy-done.13, f32[128]{0:T(128)} %get-tuple-element.1699, ...), channel_id=1, replica_groups=mesh['rounds'=8,'tiles'=32] {'tiles'}, use_global_device_ids=true, to_apply=%region_19.20 | all-reduce | flops 897 | bytes 7176 | tf_op jit(solution)/shard_map/psum | solution.py:230
  873.7 18.1 %all-reduce.4 = (f32[512]{0:T(512)}, f32[128]{0:T(128)}, f32[128]{0:T(128)}, f32[128]{0:T(128)}, f32[]{:T(128)}) all-reduce(f32[512]{0:T(512)S(1)} %get-tuple-element.1090, f32[128]{0:T(128)S(1)} %get-tuple-element.1091, f32[128]{0:T(128)S(1)} %get-tuple-element.1092, ...), channel_id=1, replica_groups=mesh['rounds'=8,'tiles'=32] {'rounds'}, use_global_device_ids=true, to_apply=%region_20.21 | all-reduce | flops 897 | bytes 7176 | tf_op jit(solution)/shard_map/psum | solution.py:230
  893.5 76.9 %all-reduce.13.cloned.1.call-done = f32[3,3,128,512]{3,2,1,0:T(8,128)} async-done(((f32[3,3,128,512]{3,2,1,0:T(8,128)}), f32[3,3,128,512]{3,2,1,0:T(8,128)}) %all-reduce.13.cloned.1.call-update) | async-done | bytes 2359312 | tf_op jit(solution)/shard_map/psum | solution.py:230
  (1206 shorter events, 421.6 us)
Async XLA Ops:
  7.2 803.5 %all-reduce.11.cloned.1.call-start = ((), (), s32[]{:S(2)}) async-start(), calls=%async_computation | async-start | bytes 4718592 | tf_op jit(solution)/shard_map/psum | solution.py:230
  190.4 15.2 %collective-permute-start.2 = (bf16[1,1,64,512]{3,2,1,0:T(8,128)(2,1)}, bf16[1,1,64,512]{3,2,1,0:T(8,128)(2,1)}, u32[]{:S(2)}, u32[]{:S(2)}) collective-permute-start(bf16[1,1,64,512]{3,2,1,0:T(8,128)(2,1)} %get-tuple-element.1499), channel_id=1, source_target_pairs={{1,0},{2,1},{3,2},{4,3},{5,4},{6,5},{7,6},{8,7},{9,8},{10,9},{11,1... | collective-permute-start | bytes 196616 | tf_op jit(solution)/shard_map/while/body/eval_jaxpr/while/body/eval_jaxpr/ppermute | solution.py:18
  196.4 9.2 collective-permute-start.3
  211.0 12.8 %collective-permute-start.2 = (bf16[1,1,64,512]{3,2,1,0:T(8,128)(2,1)}, bf16[1,1,64,512]{3,2,1,0:T(8,128)(2,1)}, u32[]{:S(2)}, u32[]{:S(2)}) collective-permute-start(bf16[1,1,64,512]{3,2,1,0:T(8,128)(2,1)} %get-tuple-element.1499), channel_id=1, source_target_pairs={{1,0},{2,1},{3,2},{4,3},{5,4},{6,5},{7,6},{8,7},{9,8},{10,9},{11,1... | collective-permute-start | bytes 196616 | tf_op jit(solution)/shard_map/while/body/eval_jaxpr/while/body/eval_jaxpr/ppermute | solution.py:18
  229.3 12.9 %collective-permute-start.2 = (bf16[1,1,64,512]{3,2,1,0:T(8,128)(2,1)}, bf16[1,1,64,512]{3,2,1,0:T(8,128)(2,1)}, u32[]{:S(2)}, u32[]{:S(2)}) collective-permute-start(bf16[1,1,64,512]{3,2,1,0:T(8,128)(2,1)} %get-tuple-element.1499), channel_id=1, source_target_pairs={{1,0},{2,1},{3,2},{4,3},{5,4},{6,5},{7,6},{8,7},{9,8},{10,9},{11,1... | collective-permute-start | bytes 196616 | tf_op jit(solution)/shard_map/while/body/eval_jaxpr/while/body/eval_jaxpr/ppermute | solution.py:18
  232.9 9.2 collective-permute-start.3
  247.6 12.8 %collective-permute-start.2 = (bf16[1,1,64,512]{3,2,1,0:T(8,128)(2,1)}, bf16[1,1,64,512]{3,2,1,0:T(8,128)(2,1)}, u32[]{:S(2)}, u32[]{:S(2)}) collective-permute-start(bf16[1,1,64,512]{3,2,1,0:T(8,128)(2,1)} %get-tuple-element.1499), channel_id=1, source_target_pairs={{1,0},{2,1},{3,2},{4,3},{5,4},{6,5},{7,6},{8,7},{9,8},{10,9},{11,1... | collective-permute-start | bytes 196616 | tf_op jit(solution)/shard_map/while/body/eval_jaxpr/while/body/eval_jaxpr/ppermute | solution.py:18
  251.2 9.2 collective-permute-start.3
  265.8 12.8 %collective-permute-start.2 = (bf16[1,1,64,512]{3,2,1,0:T(8,128)(2,1)}, bf16[1,1,64,512]{3,2,1,0:T(8,128)(2,1)}, u32[]{:S(2)}, u32[]{:S(2)}) collective-permute-start(bf16[1,1,64,512]{3,2,1,0:T(8,128)(2,1)} %get-tuple-element.1499), channel_id=1, source_target_pairs={{1,0},{2,1},{3,2},{4,3},{5,4},{6,5},{7,6},{8,7},{9,8},{10,9},{11,1... | collective-permute-start | bytes 196616 | tf_op jit(solution)/shard_map/while/body/eval_jaxpr/while/body/eval_jaxpr/ppermute | solution.py:18
  269.5 9.2 collective-permute-start.3
  284.0 12.8 %collective-permute-start.2 = (bf16[1,1,64,512]{3,2,1,0:T(8,128)(2,1)}, bf16[1,1,64,512]{3,2,1,0:T(8,128)(2,1)}, u32[]{:S(2)}, u32[]{:S(2)}) collective-permute-start(bf16[1,1,64,512]{3,2,1,0:T(8,128)(2,1)} %get-tuple-element.1499), channel_id=1, source_target_pairs={{1,0},{2,1},{3,2},{4,3},{5,4},{6,5},{7,6},{8,7},{9,8},{10,9},{11,1... | collective-permute-start | bytes 196616 | tf_op jit(solution)/shard_map/while/body/eval_jaxpr/while/body/eval_jaxpr/ppermute | solution.py:18
  287.7 9.2 collective-permute-start.3
  302.3 12.8 %collective-permute-start.2 = (bf16[1,1,64,512]{3,2,1,0:T(8,128)(2,1)}, bf16[1,1,64,512]{3,2,1,0:T(8,128)(2,1)}, u32[]{:S(2)}, u32[]{:S(2)}) collective-permute-start(bf16[1,1,64,512]{3,2,1,0:T(8,128)(2,1)} %get-tuple-element.1499), channel_id=1, source_target_pairs={{1,0},{2,1},{3,2},{4,3},{5,4},{6,5},{7,6},{8,7},{9,8},{10,9},{11,1... | collective-permute-start | bytes 196616 | tf_op jit(solution)/shard_map/while/body/eval_jaxpr/while/body/eval_jaxpr/ppermute | solution.py:18
  305.9 9.2 collective-permute-start.3
  320.6 12.9 %collective-permute-start.2 = (bf16[1,1,64,512]{3,2,1,0:T(8,128)(2,1)}, bf16[1,1,64,512]{3,2,1,0:T(8,128)(2,1)}, u32[]{:S(2)}, u32[]{:S(2)}) collective-permute-start(bf16[1,1,64,512]{3,2,1,0:T(8,128)(2,1)} %get-tuple-element.1499), channel_id=1, source_target_pairs={{1,0},{2,1},{3,2},{4,3},{5,4},{6,5},{7,6},{8,7},{9,8},{10,9},{11,1... | collective-permute-start | bytes 196616 | tf_op jit(solution)/shard_map/while/body/eval_jaxpr/while/body/eval_jaxpr/ppermute | solution.py:18
  324.2 9.2 collective-permute-start.3
  529.8 15.2 %collective-permute-start.2 = (bf16[1,1,64,512]{3,2,1,0:T(8,128)(2,1)}, bf16[1,1,64,512]{3,2,1,0:T(8,128)(2,1)}, u32[]{:S(2)}, u32[]{:S(2)}) collective-permute-start(bf16[1,1,64,512]{3,2,1,0:T(8,128)(2,1)} %get-tuple-element.1499), channel_id=1, source_target_pairs={{1,0},{2,1},{3,2},{4,3},{5,4},{6,5},{7,6},{8,7},{9,8},{10,9},{11,1... | collective-permute-start | bytes 196616 | tf_op jit(solution)/shard_map/while/body/eval_jaxpr/while/body/eval_jaxpr/ppermute | solution.py:18
  535.8 9.2 collective-permute-start.3
  550.4 12.8 %collective-permute-start.2 = (bf16[1,1,64,512]{3,2,1,0:T(8,128)(2,1)}, bf16[1,1,64,512]{3,2,1,0:T(8,128)(2,1)}, u32[]{:S(2)}, u32[]{:S(2)}) collective-permute-start(bf16[1,1,64,512]{3,2,1,0:T(8,128)(2,1)} %get-tuple-element.1499), channel_id=1, source_target_pairs={{1,0},{2,1},{3,2},{4,3},{5,4},{6,5},{7,6},{8,7},{9,8},{10,9},{11,1... | collective-permute-start | bytes 196616 | tf_op jit(solution)/shard_map/while/body/eval_jaxpr/while/body/eval_jaxpr/ppermute | solution.py:18
  568.6 12.9 %collective-permute-start.2 = (bf16[1,1,64,512]{3,2,1,0:T(8,128)(2,1)}, bf16[1,1,64,512]{3,2,1,0:T(8,128)(2,1)}, u32[]{:S(2)}, u32[]{:S(2)}) collective-permute-start(bf16[1,1,64,512]{3,2,1,0:T(8,128)(2,1)} %get-tuple-element.1499), channel_id=1, source_target_pairs={{1,0},{2,1},{3,2},{4,3},{5,4},{6,5},{7,6},{8,7},{9,8},{10,9},{11,1... | collective-permute-start | bytes 196616 | tf_op jit(solution)/shard_map/while/body/eval_jaxpr/while/body/eval_jaxpr/ppermute | solution.py:18
  572.3 9.2 collective-permute-start.3
  586.9 12.8 %collective-permute-start.2 = (bf16[1,1,64,512]{3,2,1,0:T(8,128)(2,1)}, bf16[1,1,64,512]{3,2,1,0:T(8,128)(2,1)}, u32[]{:S(2)}, u32[]{:S(2)}) collective-permute-start(bf16[1,1,64,512]{3,2,1,0:T(8,128)(2,1)} %get-tuple-element.1499), channel_id=1, source_target_pairs={{1,0},{2,1},{3,2},{4,3},{5,4},{6,5},{7,6},{8,7},{9,8},{10,9},{11,1... | collective-permute-start | bytes 196616 | tf_op jit(solution)/shard_map/while/body/eval_jaxpr/while/body/eval_jaxpr/ppermute | solution.py:18
  590.6 9.2 collective-permute-start.3
  605.2 12.8 %collective-permute-start.2 = (bf16[1,1,64,512]{3,2,1,0:T(8,128)(2,1)}, bf16[1,1,64,512]{3,2,1,0:T(8,128)(2,1)}, u32[]{:S(2)}, u32[]{:S(2)}) collective-permute-start(bf16[1,1,64,512]{3,2,1,0:T(8,128)(2,1)} %get-tuple-element.1499), channel_id=1, source_target_pairs={{1,0},{2,1},{3,2},{4,3},{5,4},{6,5},{7,6},{8,7},{9,8},{10,9},{11,1... | collective-permute-start | bytes 196616 | tf_op jit(solution)/shard_map/while/body/eval_jaxpr/while/body/eval_jaxpr/ppermute | solution.py:18
  623.4 12.8 %collective-permute-start.2 = (bf16[1,1,64,512]{3,2,1,0:T(8,128)(2,1)}, bf16[1,1,64,512]{3,2,1,0:T(8,128)(2,1)}, u32[]{:S(2)}, u32[]{:S(2)}) collective-permute-start(bf16[1,1,64,512]{3,2,1,0:T(8,128)(2,1)} %get-tuple-element.1499), channel_id=1, source_target_pairs={{1,0},{2,1},{3,2},{4,3},{5,4},{6,5},{7,6},{8,7},{9,8},{10,9},{11,1... | collective-permute-start | bytes 196616 | tf_op jit(solution)/shard_map/while/body/eval_jaxpr/while/body/eval_jaxpr/ppermute | solution.py:18
  627.1 9.2 collective-permute-start.3
  641.7 12.8 %collective-permute-start.2 = (bf16[1,1,64,512]{3,2,1,0:T(8,128)(2,1)}, bf16[1,1,64,512]{3,2,1,0:T(8,128)(2,1)}, u32[]{:S(2)}, u32[]{:S(2)}) collective-permute-start(bf16[1,1,64,512]{3,2,1,0:T(8,128)(2,1)} %get-tuple-element.1499), channel_id=1, source_target_pairs={{1,0},{2,1},{3,2},{4,3},{5,4},{6,5},{7,6},{8,7},{9,8},{10,9},{11,1... | collective-permute-start | bytes 196616 | tf_op jit(solution)/shard_map/while/body/eval_jaxpr/while/body/eval_jaxpr/ppermute | solution.py:18
  645.3 9.2 collective-permute-start.3
  660.0 12.9 %collective-permute-start.2 = (bf16[1,1,64,512]{3,2,1,0:T(8,128)(2,1)}, bf16[1,1,64,512]{3,2,1,0:T(8,128)(2,1)}, u32[]{:S(2)}, u32[]{:S(2)}) collective-permute-start(bf16[1,1,64,512]{3,2,1,0:T(8,128)(2,1)} %get-tuple-element.1499), channel_id=1, source_target_pairs={{1,0},{2,1},{3,2},{4,3},{5,4},{6,5},{7,6},{8,7},{9,8},{10,9},{11,1... | collective-permute-start | bytes 196616 | tf_op jit(solution)/shard_map/while/body/eval_jaxpr/while/body/eval_jaxpr/ppermute | solution.py:18
  663.6 9.2 collective-permute-start.3
  675.8 216.1 %all-reduce.15.cloned.1.call-start = ((), (), s32[]{:S(2)}) async-start(), calls=%async_computation.2 | async-start | bytes 262144 | tf_op jit(solution)/shard_map/psum | solution.py:229
  677.5 293.0 %all-reduce.13.cloned.1.call-start = ((), (), s32[]{:S(2)}) async-start(), calls=%async_computation.1 | async-start | bytes 4718592 | tf_op jit(solution)/shard_map/psum | solution.py:230
  (215 other events, 1201.1 us)
Sparse Core Ops, SparseCore 0:
  675.9 134.6 all-reduce.10
  813.0 72.8 all-reduce.14
  888.3 82.1 all-reduce.12
